TPU v7x, 32 devices: a whole 2x2x4 slice. The times are simulated.
32 devices in a mesh: fsdp: 8 (over y, x, core), dp: 4 (over z).
Axes of the slice: x: 2, y: 2, z: 4, core: 2. Of those that a mesh axis runs over, the one named last changes fastest.
Arguments:
- hidden: bfloat16 [8192, 14336], P(('fsdp', 'dp')), may hold values from -6 to 6
- cotangent: bfloat16 [8192, 4096], P(('fsdp', 'dp')), may hold values from -6 to 6
- tiles: bfloat16 [64, 128, 128], P('fsdp'), may hold values from -0.25 to 0.25
- tile_rows: int32 [64], P('fsdp'), may hold values from 0 to 111, as said below
- tile_cols: int32 [64], P('fsdp'), may hold values from 0 to 31, as said below
- counts: int32 [8], P('fsdp'), may hold values from 1 to 8, as said below
Outputs:
- layer_out: bfloat16 [8192, 4096], P(('fsdp', 'dp'))
- hidden_grad: bfloat16 [8192, 14336], P(('fsdp', 'dp'))
- weight_grad: float32 [64, 128, 128], P('fsdp')
Inputs may be any that keep to these rules, and one draw needn't show every extreme that they name: `tile_rows`: every slot (live or not) names a different block; the row block is below 112. `tile_cols`: the column block is below 32. `counts`: some owner has all 8 slots live in every draw.
All inputs are finite; a program needn't handle non-finite values.
Results may differ from a plain program's by a relative error of at most 0.0085.
Values may be sent and summed in bfloat16 or wider, within the bound.
A program may use at most 192 MiB of HBM per device.

v0:
```python
import math
import jax
import jax.numpy as jnp
from jax import lax
from jax.sharding import PartitionSpec as P


def one_hot_of(ids, width):
    return (ids[:, None] == jnp.arange(width, dtype=jnp.int32)[None, :]).astype(jnp.bfloat16)


def select_blocks(blocks, ids):
    table = one_hot_of(ids, blocks.shape[1])
    chosen = jnp.einsum("tbe,kb->tke", blocks, table, preferred_element_type=jnp.float32)
    return chosen.astype(jnp.bfloat16)


def place_blocks(partial_value, ids, width):
    table = one_hot_of(ids, width).astype(jnp.float32)
    return jnp.einsum("tke,kb->tbe", partial_value, table)


def shards(hidden, cotangent, tiles, tile_rows, tile_cols, counts):
    tokens = hidden.shape[0]
    slots_own = tiles.shape[0]
    edge_len = tiles.shape[1]
    blocks_ff = hidden.shape[1] // edge_len
    blocks_model = cotangent.shape[1] // edge_len
    live_slots = jnp.arange(slots_own) < counts[0]
    masked = jnp.where(live_slots[:, None, None], tiles, jnp.zeros_like(tiles))
    all_rows, all_cols = (
        lax.all_gather(tile_rows, "fsdp", axis=0, tiled=True),
        lax.all_gather(tile_cols, "fsdp", axis=0, tiled=True),
    )
    hidden_blocks = hidden.reshape(tokens, blocks_ff, edge_len)
    upstream_blocks = cotangent.reshape(tokens, blocks_model, edge_len)
    gathered = lax.all_gather(masked, "fsdp", axis=0, tiled=True)
    row_ids = all_rows
    col_ids = all_cols
    picked = select_blocks(hidden_blocks, row_ids)
    partial_value = jnp.einsum("tkf,kfd->tkd", picked, gathered, preferred_element_type=jnp.float32)
    layer_acc = place_blocks(partial_value, col_ids, blocks_model)
    row_ids = all_rows
    col_ids = all_cols
    upstream = select_blocks(upstream_blocks, col_ids)
    partial_value = jnp.einsum(
        "tkd,kfd->tkf", upstream, gathered, preferred_element_type=jnp.float32
    )
    grad_acc = place_blocks(partial_value, row_ids, blocks_ff)
    row_ids = all_rows
    col_ids = all_cols
    picked = select_blocks(hidden_blocks, row_ids)
    upstream = select_blocks(upstream_blocks, col_ids)
    owned = lax.psum_scatter(
        jnp.einsum("tkf,tkd->kfd", picked, upstream, preferred_element_type=jnp.float32),
        "fsdp",
        scatter_dimension=0,
        tiled=True,
    )
    summed = lax.psum(owned, "dp")
    raw_grad = jnp.where(live_slots[:, None, None], summed, jnp.zeros_like(summed))
    local_squares = jnp.sum(raw_grad * raw_grad)
    local_entries = counts[0].astype(jnp.float32) * edge_len * edge_len
    squares, entries = lax.psum((local_squares, local_entries), "fsdp")
    spread = jnp.sqrt(squares / entries)
    root_tokens = math.sqrt(tokens * lax.axis_size("fsdp") * lax.axis_size("dp"))
    factor = jnp.minimum(1.0, 0.5 * root_tokens / spread) / root_tokens
    layer_out = layer_acc.reshape(tokens, blocks_model * edge_len).astype(jnp.bfloat16)
    hidden_grad = grad_acc.reshape(tokens, blocks_ff * edge_len).astype(jnp.bfloat16)
    return (layer_out, hidden_grad, raw_grad * factor)


def solution(mesh):
    placed = (
        P(("fsdp", "dp"), None),
        P(("fsdp", "dp"), None),
        P("fsdp", None, None),
        P("fsdp"),
        P("fsdp"),
        P("fsdp"),
    )
    return jax.shard_map(
        shards,
        mesh=mesh,
        in_specs=placed,
        out_specs=(P(("fsdp", "dp"), None), P(("fsdp", "dp"), None), P("fsdp", None, None)),
        check_vma=False,
    )
```

profile of v0, /device:TPU:0, one launch (start us, length us, event | category | flops | bytes accessed | tf_op | source)
XLA Modules:
  0.0 171.5 jit_solution(11835242717945344327)
XLA Ops:
  7.2 0.0 all-gather.2.cloned.1.call-start
  7.9 1.7 %broadcast_select_fusion = bf16[8,128,128]{2,1,0:T(8,128)(2,1)} fusion(bf16[8,128,128]{2,1,0:T(8,128)(2,1)} %param.8, pred[8]{0:T(512)(128)(4,1)S(1)} %iota_compare_fusion.2), kind=kLoop, calls=%fused_computation.16 | loop fusion | flops 131072 | bytes 524296 | tf_op jit(solution)/shard_map/jit(_where)/select_n | solution.py:30
  9.6 0.0 all-gather.2.cloned.1.call-update
  9.6 0.0 reduce-scatter.2.cloned.1.call-start
  9.7 0.0 copy-start.8
  9.7 0.0 copy-start.6
  9.7 0.0 copy-start.7
  9.7 7.8 %copy.16 = bf16[32,8,112,128]{3,2,1,0:T(8,128)(2,1)} copy(bf16[32,8,112,128]{3,1,2,0:T(8,128)(2,1)} %bitcast.50) | data formatting | bytes 14680064
  17.6 0.0 copy-done.8
  17.6 0.6 dynamic-slice
  18.7 0.0 copy-done.6
  18.7 0.2 dynamic-update-slice
  19.0 0.0 copy-done.7
  19.0 0.2 dynamic-update-slice.1
  19.2 9.7 %all-reduce.2 = (s32[64]{0:T(128)S(1)}, s32[64]{0:T(128)S(1)}) all-reduce(s32[64]{0:T(128)S(1)} %dynamic-update-slice.1, s32[64]{0:T(128)S(1)} %dynamic-update-slice), channel_id=1, replica_groups=mesh['fsdp'=8,'dp'=4] {'fsdp'}, use_global_device_ids=true, to_apply=%add.1 | all-reduce | flops 128 | bytes 1024
  28.9 6.4 %convert_bitcast_fusion.1 = bf16[256,64,128]{2,1,0:T(8,128)(2,1)} fusion(bf16[256,112,128]{2,1,0:T(8,128)(2,1)} %bitcast.46, s32[64]{0:T(128)S(1)} %get-tuple-element.3), kind=kOutput, calls=%fused_computation.7 | convolution fusion | flops 471866368 | bytes 11534592 | tf_op jit(solution)/shard_map/tbe,kb->tke/dot_general | solution.py:14
  35.3 0.0 copy-start.5
  35.3 7.1 %copy.11 = bf16[256,64,128]{0,2,1:T(8,128)(2,1)} copy(bf16[256,64,128]{2,1,0:T(8,128)(2,1)} %convert_bitcast_fusion.1) | data formatting | bytes 8388608 | tf_op jit(solution)/shard_map/convert_element_type | solution.py:15
  42.3 0.0 copy-done.5
  42.3 0.5 copy.18
  42.8 0.0 copy-start
  42.8 1.3 convert_bitcast_fusion
  44.1 0.0 copy-start.1
  44.1 2.0 %copy-done.1 = bf16[256,64,128]{2,1,0:T(8,128)(2,1)} copy-done((bf16[256,64,128]{2,1,0:T(8,128)(2,1)}, bf16[256,64,128]{2,1,0:T(8,128)(2,1)S(1)}, u32[]{:S(2)}) %copy-start.1) | copy-done | bytes 4194328
  46.1 0.0 copy-done
  46.1 7.2 %fusion.9 = f32[64,128,128]{2,1,0:T(8,128)} fusion(bf16[256,64,128]{0,2,1:T(8,128)(2,1)S(1)} %copy-done, bf16[256,64,128]{2,1,0:T(8,128)(2,1)S(1)} %convert_bitcast_fusion), kind=kOutput, calls=%fused_computation.10 | convolution fusion | flops 536870912 | bytes 12582912 | tf_op jit(solution)/shard_map/tkf,tkd->kfd/dot_general | solution.py:55
  53.3 0.0 reduce-scatter.2.cloned.1.call-update
  53.4 0.2 all-reduce.6.cloned.1.call-start
  53.6 0.0 all-gather.2.cloned.1.call-done
  53.6 9.4 %fusion.7 = bf16[64,128,256]{2,1,0:T(8,128)(2,1)} fusion(bf16[64,128,128]{2,1,0:T(8,128)(2,1)} %all-gather.2.cloned.1.call-done, bf16[256,64,128]{2,1,0:T(8,128)(2,1)} %copy-done.1), kind=kOutput, calls=%fused_computation.8 | convolution fusion | flops 536870912 | bytes 10485760 | tf_op jit(solution)/shard_map/tkd,kfd->tkf/dot_general | solution.py:46
  63.0 6.6 %copy.15 = bf16[64,128,256]{1,0,2:T(8,128)(2,1)} copy(bf16[64,128,256]{2,1,0:T(8,128)(2,1)} %fusion.7) | data formatting | bytes 8388608 | tf_op jit(solution)/shard_map/tkd,kfd->tkf/dot_general | solution.py:46
  69.7 0.0 copy-start.3
  69.7 7.6 %fusion.4 = bf16[112,256,128]{2,0,1:T(8,128)(2,1)} fusion(bf16[64,128,256]{1,0,2:T(8,128)(2,1)} %copy.15, s32[64]{0:T(128)S(1)} %get-tuple-element.3), kind=kOutput, calls=%fused_computation.5 | convolution fusion | flops 469769216 | bytes 11534592 | tf_op jit(solution)/shard_map/tke,kb->tbe/dot_general | solution.py:20
  77.3 26.8 %reduce-scatter.2.cloned.1.call-done = f32[8,128,128]{2,1,0:T(8,128)} async-done(((f32[64,128,128]{2,1,0:T(8,128)}), f32[8,128,128]{2,1,0:T(8,128)}) %reduce-scatter.2.cloned.1.call-update) | async-done | bytes 524304 | tf_op jit(solution)/shard_map/reduce_scatter | solution.py:54
  104.1 0.0 all-reduce.6.cloned.1.call-update
  104.1 0.0 copy-done.3
  104.1 0.0 copy-start.2
  104.1 5.6 %fusion.24 = bf16[64,128,256]{2,1,0:T(8,128)(2,1)} fusion(bf16[64,128,128]{2,1,0:T(8,128)(2,1)S(1)} %copy-done.3, bf16[256,64,128]{0,2,1:T(8,128)(2,1)} %copy.11), kind=kOutput, calls=%fused_computation.26 | convolution fusion | flops 536870912 | bytes 10485760 | tf_op jit(solution)/shard_map/tkf,kfd->tkd/dot_general | solution.py:41
  109.8 0.0 copy-done.2
  109.8 4.9 %copy.26 = bf16[32,8,112,128]{3,1,2,0:T(8,128)(2,1)} copy(bf16[32,8,112,128]{3,2,1,0:T(8,128)(2,1)S(1)} %bitcast.47) | data formatting | bytes 14680064
  114.7 6.5 %copy.13 = bf16[64,128,256]{1,0,2:T(8,128)(2,1)} copy(bf16[64,128,256]{2,1,0:T(8,128)(2,1)} %fusion.24) | data formatting | bytes 8388608 | tf_op jit(solution)/shard_map/tkf,kfd->tkd/dot_general | solution.py:41
  121.2 2.9 %fusion.11 = bf16[32,256,128]{2,0,1:T(8,128)(2,1)S(1)} fusion(bf16[64,128,256]{1,0,2:T(8,128)(2,1)} %copy.13, s32[64]{0:T(128)S(1)} %get-tuple-element.4), kind=kOutput, calls=%fused_computation.13 | convolution fusion | flops 134219776 | bytes 6291712 | tf_op jit(solution)/shard_map/tke,kb->tbe/dot_general | solution.py:20
  124.1 21.0 %all-reduce.6.cloned.1.call-done = f32[8,128,128]{2,1,0:T(8,128)} async-done(((f32[8,128,128]{2,1,0:T(8,128)}), f32[8,128,128]{2,1,0:T(8,128)}) %all-reduce.6.cloned.1.call-update) | async-done | bytes 524304 | tf_op jit(solution)/shard_map/psum | solution.py:60
  145.2 1.9 %multiply_reduce_fusion = f32[]{:T(128)} fusion(f32[8,128,128]{2,1,0:T(8,128)} %all-reduce.6.cloned.1.call-done, pred[8]{0:T(512)(128)(4,1)S(1)} %iota_compare_fusion.2), kind=kLoop, calls=%fused_computation.14 | loop fusion | flops 393215 | bytes 524300 | tf_op jit(solution)/shard_map/reduce_sum | solution.py:62
  147.1 2.3 %copy.27 = bf16[32,8,32,128]{3,1,2,0:T(8,128)(2,1)} copy(bf16[32,8,32,128]{3,2,1,0:T(8,128)(2,1)S(1)} %bitcast.48) | data formatting | bytes 4194304
  149.4 13.3 %all-reduce.3 = (f32[]{:T(128)}, f32[]{:T(128)}) all-reduce(f32[]{:T(128)} %multiply_reduce_fusion, f32[]{:T(128)S(6)} %mul.14), channel_id=1, replica_groups=mesh['fsdp'=8,'dp'=4] {'fsdp'}, use_global_device_ids=true, to_apply=%region_3.4 | all-reduce | flops 2 | bytes 16 | tf_op jit(solution)/shard_map/psum | solution.py:64
  164.0 0.0 copy-done.4
  164.0 0.9 select_multiply_fusion
  (4 shorter events, 0.0 us)
Async XLA Ops:
  7.2 46.5 %all-gather.2.cloned.1.call-start = ((), (), s32[]{:S(2)}) async-start(), calls=%async_computation.1 | async-start | bytes 2359296 | tf_op jit(solution)/shard_map/all_gather | solution.py:37
  9.6 94.5 %reduce-scatter.2.cloned.1.call-start = ((), (), s32[]{:S(2)}) async-start(), calls=%async_computation.2 | async-start | bytes 4718592 | tf_op jit(solution)/shard_map/reduce_scatter | solution.py:54
  9.7 7.9 %copy-start.8 = (u32[32]{0:T(128)S(1)}, u32[32]{0:T(128)}, u32[]{:S(2)}) copy-start(u32[32]{0:T(128)} %constant.18) | copy-start | bytes 388
  9.7 9.0 %copy-start.6 = (s32[8]{0:T(128)S(1)}, s32[8]{0:T(128)}, u32[]{:S(2)}) copy-start(s32[8]{0:T(128)} %param.10) | copy-start | bytes 100
  9.7 9.3 %copy-start.7 = (s32[8]{0:T(128)S(1)}, s32[8]{0:T(128)}, u32[]{:S(2)}) copy-start(s32[8]{0:T(128)} %param.9) | copy-start | bytes 100
  35.3 7.1 %copy-start.5 = (bf16[256,4096]{1,0:T(8,128)(2,1)S(1)}, bf16[256,4096]{1,0:T(8,128)(2,1)}, u32[]{:S(2)}) copy-start(bf16[256,4096]{1,0:T(8,128)(2,1)} %param.7) | copy-start | bytes 6291460
  42.8 3.3 %copy-start = (bf16[256,64,128]{0,2,1:T(8,128)(2,1)S(1)}, bf16[256,64,128]{0,2,1:T(8,128)(2,1)}, u32[]{:S(2)}) copy-start(bf16[256,64,128]{0,2,1:T(8,128)(2,1)} %copy.11) | copy-start | bytes 12582916
  44.1 2.0 %copy-start.1 = (bf16[256,64,128]{2,1,0:T(8,128)(2,1)}, bf16[256,64,128]{2,1,0:T(8,128)(2,1)S(1)}, u32[]{:S(2)}) copy-start(bf16[256,64,128]{2,1,0:T(8,128)(2,1)S(1)} %convert_bitcast_fusion) | copy-start | bytes 12582916
  53.4 91.8 %all-reduce.6.cloned.1.call-start = ((), (), s32[]{:S(2)}) async-start(), calls=%async_computation.3 | async-start | bytes 1048576 | tf_op jit(solution)/shard_map/psum | solution.py:60
  69.7 34.5 %copy-start.3 = (bf16[64,128,128]{2,1,0:T(8,128)(2,1)S(1)}, bf16[64,128,128]{2,1,0:T(8,128)(2,1)}, u32[]{:S(2)}) copy-start(bf16[64,128,128]{2,1,0:T(8,128)(2,1)} %all-gather.2.cloned.1.call-done) | copy-start | bytes 6291460
  104.1 5.6 %copy-start.2 = (bf16[112,256,128]{2,0,1:T(8,128)(2,1)S(1)}, bf16[112,256,128]{2,0,1:T(8,128)(2,1)}, u32[]{:S(2)}) copy-start(bf16[112,256,128]{2,0,1:T(8,128)(2,1)} %fusion.4) | copy-start | bytes 22020100
  145.2 18.9 %copy-start.4 = (f32[8,128,128]{2,1,0:T(8,128)S(1)}, f32[8,128,128]{2,1,0:T(8,128)}, u32[]{:S(2)}) copy-start(f32[8,128,128]{2,1,0:T(8,128)} %all-reduce.6.cloned.1.call-done) | copy-start | bytes 1572868
Sparse Core Ops, SparseCore 0:
  10.4 30.5 all-gather.1
  53.5 50.5 reduce-scatter.1
  106.4 38.6 all-reduce.5
where the time goes:
time: 172 us; the launch traced here: 171 us
  waiting for transfers between devices  47.9 us (28%)
  matrix products  40.4 us (23%)
  local copies, waits for them, and re-layouts  38.9 us (23%)
  blocking collectives  23 us (13%)
  between operations  16.4 us (10%)
  other arithmetic  4.57 us (3%)
    reduce_scatter x1, waiting for transfers between devices, shards(): lax.psum_scatter(jnp.einsum('tkf,tkd->kfd', picked, upstream, preferred_e...  26.8 us
    psum x1, waiting for transfers between devices, shards(): summed = lax.psum(owned, 'dp')  21 us
    unnamed x27, local copies, waits for them, and re-layouts  18.6 us
    psum x1, blocking collectives, shards(): squares, entries = lax.psum((local_squares, local_entries), 'fsdp')  13.3 us
    dot_general x2, matrix products, place_blocks(): return jnp.einsum('tke,kb->tbe', partial_value, table)  10.5 us
    unnamed x1, blocking collectives  9.69 us
    dot_general x1, matrix products, shards(): jnp.einsum('tkd,kfd->tkf', upstream, gathered, preferred_element_type=jnp...  9.41 us
    dot_general x2, matrix products, select_blocks(): jnp.einsum('tbe,kb->tke', blocks, table, preferred_element_type=jnp.float32)  7.66 us
  transfers between devices with their start and end apart: 3, of which 2 were waited for; matrix products, arithmetic and copies ran while one was open for 44% of the time, Pallas kernels for 0%

commit v1 on v0

--- a/solution.py
+++ b/solution.py
@@ -57,7 +57,7 @@
         scatter_dimension=0,
         tiled=True,
     )
-    summed = lax.psum(owned, "dp")
+    summed = jnp.sum(lax.all_gather(owned, "dp"), axis=0)
     raw_grad = jnp.where(live_slots[:, None, None], summed, jnp.zeros_like(summed))
     local_squares = jnp.sum(raw_grad * raw_grad)
     local_entries = counts[0].astype(jnp.float32) * edge_len * edge_len

time: 172 us -> 208 us (1.21)
  waiting for transfers between devices: 47.9 us -> 87 us
  matrix products: 40.4 us -> 36.4 us
    all_gather x1, waiting for transfers between devices: 0.02 us -> 30.2 us  [shards(): gathered = lax.all_gather(masked, 'fsdp', axis=0, tiled=True)]
    reduce_scatter x1, waiting for transfers between devices: 26.8 us -> 49 us  [shards(): lax.psum_scatter(jnp.einsum('tkf,tkd->kfd', picked, upstream, preferred_e...]
    psum x1 -> x0, waiting for transfers between devices: 21 us -> none  [shards(): summed = lax.psum(owned, 'dp')]
    all_gather x0 -> x1, waiting for transfers between devices: none -> 7.67 us  [shards(): summed = jnp.sum(lax.all_gather(owned, 'dp'), axis=0)]
    dot_general x2, matrix products: 10.5 us -> 7.26 us  [place_blocks(): return jnp.einsum('tke,kb->tbe', partial_value, table)]
    unnamed x27 -> x25, local copies, waits for them, and re-layouts: 18.6 us -> 18.8 us
  transfers between devices with their start and end apart: 3 -> 3, of which waited for: 2 -> 3; matrix products, arithmetic and copies ran while one was open for 44% -> 19% of each run, Pallas kernels for 0% -> 0%
where the time goes in v1:
time: 208 us; the launch traced here: 207 us
  waiting for transfers between devices  87 us (42%)
  local copies, waits for them, and re-layouts  39 us (19%)
  matrix products  36.4 us (18%)
  blocking collectives  23.6 us (11%)
  between operations  16.6 us (8%)
  other arithmetic  4.27 us (2%)
    reduce_scatter x1, waiting for transfers between devices, shards(): lax.psum_scatter(jnp.einsum('tkf,tkd->kfd', picked, upstream, preferred_e...  49 us
    all_gather x1, waiting for transfers between devices, shards(): gathered = lax.all_gather(masked, 'fsdp', axis=0, tiled=True)  30.2 us
    unnamed x25, local copies, waits for them, and re-layouts  18.8 us
    psum x1, blocking collectives, shards(): squares, entries = lax.psum((local_squares, local_entries), 'fsdp')  14.1 us
    unnamed x1, blocking collectives  9.49 us
    dot_general x1, matrix products, shards(): jnp.einsum('tkd,kfd->tkf', upstream, gathered, preferred_element_type=jnp...  9.42 us
    all_gather x1, waiting for transfers between devices, shards(): summed = jnp.sum(lax.all_gather(owned, 'dp'), axis=0)  7.67 us
    dot_general x2, matrix products, select_blocks(): jnp.einsum('tbe,kb->tke', blocks, table, preferred_element_type=jnp.float32)  7.64 us
  transfers between devices with their start and end apart: 3, of which 3 were waited for; matrix products, arithmetic and copies ran while one was open for 19% of the time, Pallas kernels for 0%

profile of v1, /device:TPU:0, one launch (start us, length us, event | category | flops | bytes accessed | tf_op | source)
XLA Modules:
  0.0 207.0 jit_solution(13357291266326853443)
XLA Ops:
  7.2 0.0 reduce-scatter.2.cloned.1.call-start
  7.2 0.0 copy-start.7
  7.2 0.0 copy-start.5
  7.2 0.0 copy-start.6
  7.3 7.8 %copy.16 = bf16[32,8,112,128]{3,2,1,0:T(8,128)(2,1)} copy(bf16[32,8,112,128]{3,1,2,0:T(8,128)(2,1)} %bitcast.51) | data formatting | bytes 14680064
  15.1 0.0 copy-done.7
  15.1 0.6 dynamic-slice
  16.3 0.0 copy-done.5
  16.4 0.2 dynamic-update-slice
  16.6 0.0 copy-done.6
  16.6 0.2 dynamic-update-slice.1
  16.8 9.5 %all-reduce.2 = (s32[64]{0:T(128)S(1)}, s32[64]{0:T(128)S(1)}) all-reduce(s32[64]{0:T(128)S(1)} %dynamic-update-slice.1, s32[64]{0:T(128)S(1)} %dynamic-update-slice), channel_id=1, replica_groups=mesh['fsdp'=8,'dp'=4] {'fsdp'}, use_global_device_ids=true, to_apply=%add.1 | all-reduce | flops 128 | bytes 1024
  26.3 6.3 %convert_bitcast_fusion.1 = bf16[256,64,128]{2,1,0:T(8,128)(2,1)} fusion(bf16[256,112,128]{2,1,0:T(8,128)(2,1)} %bitcast.47, s32[64]{0:T(128)S(1)} %get-tuple-element.3), kind=kOutput, calls=%fused_computation.7 | convolution fusion | flops 471866368 | bytes 11534592 | tf_op jit(solution)/shard_map/tbe,kb->tke/dot_general | solution.py:14
  32.7 0.0 copy-start.3
  32.7 7.0 %copy.11 = bf16[256,64,128]{0,2,1:T(8,128)(2,1)} copy(bf16[256,64,128]{2,1,0:T(8,128)(2,1)} %convert_bitcast_fusion.1) | data formatting | bytes 8388608 | tf_op jit(solution)/shard_map/convert_element_type | solution.py:15
  39.7 0.0 copy-done.3
  39.7 0.5 copy.18
  40.2 0.0 copy-start
  40.2 1.3 convert_bitcast_fusion
  41.5 0.0 copy-start.2
  41.5 2.0 copy-done.2
  43.5 0.0 copy-done
  43.5 7.2 %fusion.9 = f32[64,128,128]{2,1,0:T(8,128)} fusion(bf16[256,64,128]{0,2,1:T(8,128)(2,1)S(1)} %copy-done, bf16[256,64,128]{2,1,0:T(8,128)(2,1)S(1)} %convert_bitcast_fusion), kind=kOutput, calls=%fused_computation.10 | convolution fusion | flops 536870912 | bytes 12582912 | tf_op jit(solution)/shard_map/tkf,tkd->kfd/dot_general | solution.py:55
  50.7 0.0 copy-start.4
  50.7 0.0 reduce-scatter.2.cloned.1.call-update
  50.7 0.0 all-gather.4.cloned.1.call-start
  51.5 0.2 copy-done.4
  51.7 0.8 broadcast_select_fusion
  52.5 0.0 all-gather.4.cloned.1.call-update
  52.5 0.2 all-gather.6.cloned.1.call-start
  52.7 49.0 %reduce-scatter.2.cloned.1.call-done = f32[8,128,128]{2,1,0:T(8,128)} async-done(((f32[64,128,128]{2,1,0:T(8,128)}), f32[8,128,128]{2,1,0:T(8,128)}) %reduce-scatter.2.cloned.1.call-update) | async-done | bytes 524304 | tf_op jit(solution)/shard_map/reduce_scatter | solution.py:54
  101.7 0.0 all-gather.6.cloned.1.call-update
  101.8 30.2 %all-gather.4.cloned.1.call-done = bf16[64,128,128]{2,1,0:T(8,128)(2,1)} async-done(((bf16[8,128,128]{2,1,0:T(8,128)(2,1)}), bf16[64,128,128]{2,1,0:T(8,128)(2,1)}) %all-gather.4.cloned.1.call-update) | async-done | bytes 2097168 | tf_op jit(solution)/shard_map/all_gather | solution.py:37
  132.0 9.4 %fusion.7 = bf16[64,128,256]{2,1,0:T(8,128)(2,1)} fusion(bf16[64,128,128]{2,1,0:T(8,128)(2,1)} %all-gather.4.cloned.1.call-done, bf16[256,64,128]{2,1,0:T(8,128)(2,1)} %copy-done.2), kind=kOutput, calls=%fused_computation.8 | convolution fusion | flops 536870912 | bytes 10485760 | tf_op jit(solution)/shard_map/tkd,kfd->tkf/dot_general | solution.py:46
  141.4 6.5 %copy.15 = bf16[64,128,256]{1,0,2:T(8,128)(2,1)} copy(bf16[64,128,256]{2,1,0:T(8,128)(2,1)} %fusion.7) | data formatting | bytes 8388608 | tf_op jit(solution)/shard_map/tkd,kfd->tkf/dot_general | solution.py:46
  147.9 4.4 %fusion.4 = bf16[112,256,128]{2,0,1:T(8,128)(2,1)S(1)} fusion(bf16[64,128,256]{1,0,2:T(8,128)(2,1)} %copy.15, s32[64]{0:T(128)S(1)} %get-tuple-element.3), kind=kOutput, calls=%fused_computation.5 | convolution fusion | flops 469769216 | bytes 11534592 | tf_op jit(solution)/shard_map/tke,kb->tbe/dot_general | solution.py:20
  152.3 0.0 copy-start.1
  152.3 4.9 %copy.26 = bf16[32,8,112,128]{3,1,2,0:T(8,128)(2,1)} copy(bf16[32,8,112,128]{3,2,1,0:T(8,128)(2,1)S(1)} %bitcast.48) | data formatting | bytes 14680064
  157.2 0.0 copy-done.1
  157.3 4.8 %fusion.24 = bf16[64,128,256]{2,1,0:T(8,128)(2,1)} fusion(bf16[64,128,128]{2,1,0:T(8,128)(2,1)} %all-gather.4.cloned.1.call-done, bf16[256,64,128]{0,2,1:T(8,128)(2,1)S(1)} %copy-done.1), kind=kOutput, calls=%fused_computation.26 | convolution fusion | flops 536870912 | bytes 10485760 | tf_op jit(solution)/shard_map/tkf,kfd->tkd/dot_general | solution.py:41
  162.1 6.6 %copy.13 = bf16[64,128,256]{1,0,2:T(8,128)(2,1)} copy(bf16[64,128,256]{2,1,0:T(8,128)(2,1)} %fusion.24) | data formatting | bytes 8388608 | tf_op jit(solution)/shard_map/tkf,kfd->tkd/dot_general | solution.py:41
  168.7 2.9 %fusion.11 = bf16[32,256,128]{2,0,1:T(8,128)(2,1)S(1)} fusion(bf16[64,128,256]{1,0,2:T(8,128)(2,1)} %copy.13, s32[64]{0:T(128)S(1)} %get-tuple-element.4), kind=kOutput, calls=%fused_computation.13 | convolution fusion | flops 134219776 | bytes 6291712 | tf_op jit(solution)/shard_map/tke,kb->tbe/dot_general | solution.py:20
  171.6 7.7 %all-gather.6.cloned.1.call-done = f32[32,128,128]{2,1,0:T(8,128)} async-done(((f32[8,128,128]{2,1,0:T(8,128)}), f32[32,128,128]{2,1,0:T(8,128)}) %all-gather.6.cloned.1.call-update) | async-done | bytes 2097168 | tf_op jit(solution)/shard_map/all_gather | solution.py:60
  179.3 1.8 reduce_sum.18
  181.0 0.8 multiply_reduce_fusion
  181.8 2.3 %copy.27 = bf16[32,8,32,128]{3,1,2,0:T(8,128)(2,1)} copy(bf16[32,8,32,128]{3,2,1,0:T(8,128)(2,1)S(1)} %bitcast.49) | data formatting | bytes 4194304
  184.1 14.1 %all-reduce.3 = (f32[]{:T(128)}, f32[]{:T(128)}) all-reduce(f32[]{:T(128)} %multiply_reduce_fusion, f32[]{:T(128)S(6)} %mul.14), channel_id=1, replica_groups=mesh['fsdp'=8,'dp'=4] {'fsdp'}, use_global_device_ids=true, to_apply=%region_3.4 | all-reduce | flops 2 | bytes 16 | tf_op jit(solution)/shard_map/psum | solution.py:64
  199.6 0.9 select_multiply_fusion
  (3 shorter events, 0.0 us)
Async XLA Ops:
  7.2 94.6 %reduce-scatter.2.cloned.1.call-start = ((), (), s32[]{:S(2)}) async-start(), calls=%async_computation.2 | async-start | bytes 4718592 | tf_op jit(solution)/shard_map/reduce_scatter | solution.py:54
  7.2 7.9 %copy-start.7 = (u32[32]{0:T(128)S(1)}, u32[32]{0:T(128)}, u32[]{:S(2)}) copy-start(u32[32]{0:T(128)} %constant.18) | copy-start | bytes 388
  7.2 9.1 %copy-start.5 = (s32[8]{0:T(128)S(1)}, s32[8]{0:T(128)}, u32[]{:S(2)}) copy-start(s32[8]{0:T(128)} %param.10) | copy-start | bytes 100
  7.2 9.4 %copy-start.6 = (s32[8]{0:T(128)S(1)}, s32[8]{0:T(128)}, u32[]{:S(2)}) copy-start(s32[8]{0:T(128)} %param.9) | copy-start | bytes 100
  32.7 7.1 %copy-start.3 = (bf16[256,4096]{1,0:T(8,128)(2,1)S(1)}, bf16[256,4096]{1,0:T(8,128)(2,1)}, u32[]{:S(2)}) copy-start(bf16[256,4096]{1,0:T(8,128)(2,1)} %param.7) | copy-start | bytes 6291460
  40.2 3.3 %copy-start = (bf16[256,64,128]{0,2,1:T(8,128)(2,1)S(1)}, bf16[256,64,128]{0,2,1:T(8,128)(2,1)}, u32[]{:S(2)}) copy-start(bf16[256,64,128]{0,2,1:T(8,128)(2,1)} %copy.11) | copy-start | bytes 12582916
  41.5 2.0 copy-start.2
  50.7 0.9 copy-start.4
  50.7 81.3 %all-gather.4.cloned.1.call-start = ((), (), s32[]{:S(2)}) async-start(), calls=%async_computation.1 | async-start | bytes 2359296 | tf_op jit(solution)/shard_map/all_gather | solution.py:37
  52.5 126.8 %all-gather.6.cloned.1.call-start = ((), (), s32[]{:S(2)}) async-start(), calls=%async_computation.3 | async-start | bytes 2621440 | tf_op jit(solution)/shard_map/all_gather | solution.py:60
  152.3 5.0 %copy-start.1 = (bf16[256,64,128]{0,2,1:T(8,128)(2,1)S(1)}, bf16[256,64,128]{0,2,1:T(8,128)(2,1)}, u32[]{:S(2)}) copy-start(bf16[256,64,128]{0,2,1:T(8,128)(2,1)} %copy.11) | copy-start | bytes 12582916
Sparse Core Ops, SparseCore 0:
  50.9 50.8 reduce-scatter.1
  104.2 27.7 all-gather.3
  133.6 45.6 all-gather.5
